TPU v7x, 32 devices: a whole 2x2x4 slice. The times are simulated.
32 devices in a mesh: base: 16 (over z, x, core), band: 2 (over y).
Axes of the slice: x: 2, y: 2, z: 4, core: 2. Of those that a mesh axis runs over, the one named last changes fastest.
Arguments:
- coherency: float32 [16, 16, 8, 4096], P('band', None, None, 'base'), may hold values from -1.5 to 1.5
- observed: float32 [16, 8, 4096], P('band', None, 'base'), may hold values from -6 to 6
- jones_deviation: float32 [16, 16, 8, 512], P('band', None, None, 'base'), may hold values from -1.8 to 1.8
- antenna_first: int32 [4096], P('base'), may hold values from 0 to 511, as said below
- antenna_second: int32 [4096], P('base'), may hold values from 0 to 511, as said below
Outputs:
- jones: float32 [16, 16, 8, 512], P('band', None, None, 'base')
- residual: float32 [16, 8, 4096], P('band', None, 'base')
Inputs may be any that keep to these rules, and one draw needn't show every extreme that they name: `antenna_first`: every station is the first station of exactly 8 baselines. On every baseline antenna_second differs from antenna_first.
All inputs are finite; a program needn't handle non-finite values.
Results may differ from a plain program's by a relative error of at most 0.0003.
Values sent between devices are 32-bit elements; how exact they have to be, the bound alone decides.
A program may use at most 128 MiB of HBM per device.

v0:
```python
import jax
import jax.numpy as jnp
from jax import lax
from jax.sharding import PartitionSpec as P

ITERS = 3
step_gain = 1.2
penalty_gain = 0.25


def expand_matrix(packed):
    return [
        [(packed[..., 0, :], packed[..., 1, :]), (packed[..., 2, :], packed[..., 3, :])],
        [(packed[..., 4, :], packed[..., 5, :]), (packed[..., 6, :], packed[..., 7, :])],
    ]


def pack_matrix(matrix):
    return jnp.stack(
        [
            matrix[0][0][0],
            matrix[0][0][1],
            matrix[0][1][0],
            matrix[0][1][1],
            matrix[1][0][0],
            matrix[1][0][1],
            matrix[1][1][0],
            matrix[1][1][1],
        ],
        axis=-2,
    )


def complex_mul(first_term, second_term):
    return (
        first_term[0] * second_term[0] - first_term[1] * second_term[1],
        first_term[0] * second_term[1] + first_term[1] * second_term[0],
    )


def complex_add(first_term, second_term):
    return (first_term[0] + second_term[0], first_term[1] + second_term[1])


def element_of(matrix, i, j, adjoint):
    if adjoint:
        return (matrix[j][i][0], -matrix[j][i][1])
    return matrix[i][j]


def matrix_product(first_factor, second_factor, adjoint_first=False, adjoint_second=False):
    result_rows = []
    for i in range(2):
        row_items = []
        for j in range(2):
            row_items.append(
                complex_add(
                    complex_mul(
                        element_of(first_factor, i, 0, adjoint_first),
                        element_of(second_factor, 0, j, adjoint_second),
                    ),
                    complex_mul(
                        element_of(first_factor, i, 1, adjoint_first),
                        element_of(second_factor, 1, j, adjoint_second),
                    ),
                )
            )
        result_rows.append(row_items)
    return result_rows


def fit_basis(band_count):
    positions = (2.0 * jnp.arange(band_count, dtype=jnp.float32) + 1.0) / band_count - 1.0
    columns = []
    for power in range(4):
        vector = positions**power
        for earlier in columns:
            vector = vector - jnp.sum(earlier * vector) * earlier
        vector = vector / jnp.sqrt(jnp.sum(vector * vector))
        columns.append(vector)
    return jnp.stack(columns, axis=1)


def local_gradients(
    leading_rows, trailing_rows, coherency, observed, antenna_first, antenna_second, station_number
):
    leading_jones = expand_matrix(leading_rows)
    trailing_jones = expand_matrix(trailing_rows)
    sky = expand_matrix(coherency)
    model = pack_matrix(
        matrix_product(leading_jones, matrix_product(sky, trailing_jones, adjoint_second=True))
    )
    residual = observed - jnp.sum(model, axis=1)
    resid_parts = expand_matrix(residual[:, None])
    gradient_leading = pack_matrix(
        matrix_product(resid_parts, matrix_product(trailing_jones, sky, adjoint_second=True))
    )
    gradient_trailing = pack_matrix(
        matrix_product(resid_parts, matrix_product(leading_jones, sky), adjoint_first=True)
    )
    shape_out = (coherency.shape[0], coherency.shape[1], 8, station_number)
    gradient_list = (
        jnp.zeros(shape_out, jnp.float32)
        .at[:, :, :, antenna_first]
        .add(gradient_leading)
        .at[:, :, :, antenna_second]
        .add(gradient_trailing)
    )
    return (gradient_list, residual)


def per_device(coherency, observed, jones_deviation, antenna_first, antenna_second):
    highest = lax.Precision.HIGHEST
    base_count = lax.axis_size("base")
    band_count = lax.axis_size("band")
    sub_dev = coherency.shape[0]
    base_dev = coherency.shape[-1]
    own_stations = jones_deviation.shape[-1]
    station_number = own_stations * base_count
    baseline_count = base_dev * base_count
    step_size = step_gain * station_number / baseline_count
    penalty = penalty_gain * baseline_count / station_number
    poly_basis = fit_basis(sub_dev * band_count)
    local_basis = lax.dynamic_slice_in_dim(poly_basis, lax.axis_index("band") * sub_dev, sub_dev, 0)
    identity = jnp.array([1.0, 0.0, 0.0, 0.0, 0.0, 0.0, 1.0, 0.0], dtype=jnp.float32)[:, None]
    jones_current = identity + jones_deviation
    jones_current = lax.all_gather(jones_current, "base", axis=3, tiled=True)
    consensus = jones_current
    dual_var = jnp.zeros_like(jones_current)
    residual = None
    for iteration in range(ITERS):
        leading_rows = jnp.take(jones_current, antenna_first, axis=3)
        trailing_rows = jnp.take(jones_current, antenna_second, axis=3)
        local_terms, residual = local_gradients(
            leading_rows,
            trailing_rows,
            coherency,
            observed,
            antenna_first,
            antenna_second,
            station_number,
        )
        station_gradients = lax.psum(local_terms, "base")
        jones_current = jones_current + step_size * (
            station_gradients - dual_var - penalty * (jones_current - consensus)
        )
        if iteration + 1 < ITERS:
            target = jones_current + dual_var / penalty
            partial_fit = jnp.einsum("fm,fkcs->mkcs", local_basis, target, precision=highest)
            coefficients = lax.psum(partial_fit, "band")
            consensus = jnp.einsum("fm,mkcs->fkcs", local_basis, coefficients, precision=highest)
            dual_var = dual_var + penalty * (jones_current - consensus)
    jones_current = lax.dynamic_slice_in_dim(
        jones_current, lax.axis_index("base") * own_stations, own_stations, 3
    )
    return (jones_current, residual)


def solution(mesh):
    return jax.shard_map(
        per_device,
        mesh=mesh,
        in_specs=(
            P("band", None, None, "base"),
            P("band", None, "base"),
            P("band", None, None, "base"),
            P("base"),
            P("base"),
        ),
        out_specs=(P("band", None, None, "base"), P("band", None, "base")),
        check_vma=False,
    )
```

profile of v0, /device:TPU:0, one launch (start us, length us, event | category | flops | bytes accessed | tf_op | source)
XLA Modules:
  0.0 1139.3 jit_solution(16276159739745969013)
XLA Ops:
  13.6 5.7 fusion.21
  19.4 120.1 %all-gather.2.cloned.1.call-done = f32[8,16,8,512]{1,2,0,3:T(8,128)} async-done(((f32[8,16,8,32]{1,2,0,3:T(8,128)}), f32[8,16,8,512]{1,2,0,3:T(8,128)}) %all-gather.2.cloned.1.call-update) | async-done | bytes 2097168 | tf_op jit(solution)/shard_map/all_gather | solution.py:127
  139.5 11.4 copy.497
  150.9 10.6 gather_fusion
  161.5 7.1 copy.498
  168.6 10.6 gather_fusion.1
  179.3 7.6 copy.501
  200.2 5.3 fusion.20
  228.2 7.5 copy.527
  240.1 7.7 copy.536
  247.8 7.1 broadcast.414.clone
  254.8 39.8 %scatter_fusion = f32[8,16,8,512]{1,2,3,0:T(8,128)} fusion(f32[8,16,8,512]{1,2,3,0:T(8,128)} %broadcast.414.clone, s32[256]{0:T(256)S(1)} %copy-done.42, f32[256,8,16,8]{2,3,1,0:T(8,128)} %copy.527), kind=kCustom, calls=%fused_computation.6 | custom fusion | flops 262144 | bytes 3146752 | tf_op jit(solution)/shard_map/scatter-add | solution.py:105
  294.7 39.9 %scatter_fusion.1 = f32[8,16,8,512]{1,2,3,0:T(8,128)} fusion(f32[8,16,8,512]{1,2,3,0:T(8,128)} %scatter_fusion, s32[256]{0:T(256)S(1)} %copy-done.38, f32[256,8,16,8]{2,3,1,0:T(8,128)} %copy.536), kind=kCustom, calls=%fused_computation.7 | custom fusion | flops 262144 | bytes 3146752 | tf_op jit(solution)/shard_map/scatter-add | solution.py:107
  334.6 9.7 copy.537
  350.6 12.2 %copy.540 = f32[8,16,8,512]{3,0,2,1:T(8,128)} copy(f32[8,16,8,512]{1,2,0,3:T(8,128)} %all-gather.2.cloned.1.call-done) | data formatting | bytes 4194304 | tf_op jit(solution)/shard_map/all_gather | solution.py:127
  362.8 78.2 %all-reduce.6.cloned.1.call-done = f32[8,16,8,512]{3,0,2,1:T(8,128)} async-done(((f32[8,16,8,512]{3,0,2,1:T(8,128)}), f32[8,16,8,512]{3,0,2,1:T(8,128)}) %all-reduce.6.cloned.1.call-update) | async-done | bytes 2097168 | tf_op jit(solution)/shard_map/psum | solution.py:143
  443.8 7.8 copy.541
  451.6 10.8 gather_fusion.2
  462.4 10.8 gather_fusion.3
  473.2 7.1 copy.542
  481.7 7.5 copy.544
  505.4 5.2 fusion.19
  548.3 2.9 stack.26
  551.3 7.5 copy.563
  571.5 7.7 copy.572
  579.1 7.1 broadcast.414.clone.1
  586.2 39.8 %scatter_fusion.2 = f32[8,16,8,512]{1,2,3,0:T(8,128)} fusion(f32[8,16,8,512]{1,2,3,0:T(8,128)} %broadcast.414.clone.1, s32[256]{0:T(256)S(1)} %copy-done.43, f32[256,8,16,8]{2,3,1,0:T(8,128)} %copy.563), kind=kCustom, calls=%fused_computation.8 | custom fusion | flops 262144 | bytes 3146752 | tf_op jit(solution)/shard_map/scatter-add | solution.py:105
  626.0 39.8 %scatter_fusion.3 = f32[8,16,8,512]{1,2,3,0:T(8,128)} fusion(f32[8,16,8,512]{1,2,3,0:T(8,128)} %scatter_fusion.2, s32[256]{0:T(256)S(1)} %copy-done.39, f32[256,8,16,8]{2,3,1,0:T(8,128)} %copy.572), kind=kCustom, calls=%fused_computation.9 | custom fusion | flops 262144 | bytes 3146752 | tf_op jit(solution)/shard_map/scatter-add | solution.py:107
  665.8 9.7 copy.573
  686.7 86.7 %all-reduce.8.cloned.1.call-done = f32[8,16,8,512]{3,0,2,1:T(8,128)} async-done(((f32[8,16,8,512]{3,0,2,1:T(8,128)}), f32[8,16,8,512]{3,0,2,1:T(8,128)}) %all-reduce.8.cloned.1.call-update) | async-done | bytes 2097168 | tf_op jit(solution)/shard_map/psum | solution.py:143
  773.5 41.6 %all-reduce.10.cloned.1.call-done = f32[4,16,8,512]{3,0,2,1:T(4,128)} async-done(((f32[4,16,8,512]{3,0,2,1:T(4,128)}), f32[4,16,8,512]{3,0,2,1:T(4,128)}) %all-reduce.10.cloned.1.call-update) | async-done | bytes 1048592 | tf_op jit(solution)/shard_map/psum | solution.py:150
  815.0 6.0 broadcast_multiply_fusion
  821.1 7.8 copy.574
  828.8 10.8 gather_fusion.4
  839.6 10.8 gather_fusion.5
  850.4 6.3 copy.575
  856.8 6.6 copy.577
  868.5 5.2 fusion.18
  895.8 5.1 fusion.2
  908.7 4.1 stack.31
  912.8 8.4 copy.596
  926.1 7.5 copy.605
  933.6 7.1 broadcast.414
  940.7 39.8 %scatter_fusion.4 = f32[8,16,8,512]{1,2,3,0:T(8,128)} fusion(f32[8,16,8,512]{1,2,3,0:T(8,128)} %broadcast.414, s32[256]{0:T(256)S(1)} %copy-done.44, f32[256,8,16,8]{2,3,1,0:T(8,128)} %copy.596), kind=kCustom, calls=%fused_computation.10 | custom fusion | flops 262144 | bytes 3146752 | tf_op jit(solution)/shard_map/scatter-add | solution.py:105
  980.5 39.8 %scatter_fusion.5 = f32[8,16,8,512]{1,2,3,0:T(8,128)} fusion(f32[8,16,8,512]{1,2,3,0:T(8,128)} %scatter_fusion.4, s32[256]{0:T(256)S(1)} %copy-done.40, f32[256,8,16,8]{2,3,1,0:T(8,128)} %copy.605), kind=kCustom, calls=%fused_computation.11 | custom fusion | flops 262144 | bytes 3146752 | tf_op jit(solution)/shard_map/scatter-add | solution.py:107
  1020.3 10.1 copy.606
  1031.4 4.8 convolution_subtract_fusion
  1036.3 92.8 %all-reduce.12.cloned.1.call-done = f32[8,16,8,512]{3,0,2,1:T(8,128)} async-done(((f32[8,16,8,512]{3,0,2,1:T(8,128)}), f32[8,16,8,512]{3,0,2,1:T(8,128)}) %all-reduce.12.cloned.1.call-update) | async-done | bytes 2097168 | tf_op jit(solution)/shard_map/psum | solution.py:143
  (289 shorter events, 174.5 us)
Async XLA Ops:
  7.2 132.3 %all-gather.2.cloned.1.call-start = ((), (), s32[]{:S(2)}) async-start(), calls=%async_computation | async-start | bytes 17825792 | tf_op jit(solution)/shard_map/all_gather | solution.py:127
  10.2 430.8 %all-reduce.6.cloned.1.call-start = ((), (), s32[]{:S(2)}) async-start(), calls=%async_computation.1 | async-start | bytes 4194304 | tf_op jit(solution)/shard_map/psum | solution.py:143
  11.5 187.3 %copy-start.13 = (f32[8,8,256]{1,0,2:T(8,128)}, f32[8,8,256]{1,0,2:T(8,128)S(1)}, u32[]{:S(2)}) copy-start(f32[8,8,256]{1,0,2:T(8,128)S(1)} %copy.510) | copy-start | bytes 196612
  12.3 138.6 %copy-start.45 = (s32[1024]{0:T(1024)}, s32[1024]{0:T(1024)S(1)}, u32[]{:S(2)}) copy-start(s32[1024]{0:T(1024)S(1)} %pad_clamp_fusion.1) | copy-start | bytes 12292
  12.9 155.8 %copy-start.46 = (s32[1024]{0:T(1024)}, s32[1024]{0:T(1024)S(1)}, u32[]{:S(2)}) copy-start(s32[1024]{0:T(1024)S(1)} %pad_clamp_fusion) | copy-start | bytes 12292
  13.6 173.3 %copy-start.50 = (pred[256]{0:T(512)(128)(4,1)}, pred[256]{0:T(512)(128)(4,1)S(1)}, u32[]{:S(2)}) copy-start(pred[256]{0:T(512)(128)(4,1)S(1)} %get-tuple-element.206) | copy-start | bytes 772
  13.6 174.7 %copy-start.47 = (pred[256]{0:T(512)(128)(4,1)}, pred[256]{0:T(512)(128)(4,1)S(1)}, u32[]{:S(2)}) copy-start(pred[256]{0:T(512)(128)(4,1)S(1)} %get-tuple-element.205) | copy-start | bytes 772
  19.3 198.3 %copy-start.5 = (f32[8,16,1,256]{3,2,1,0:T(1,128)}, f32[8,16,1,256]{3,2,1,0:T(1,128)S(1)}, u32[]{:S(2)}) copy-start(f32[8,16,1,256]{3,2,1,0:T(1,128)S(1)} %get-tuple-element.140) | copy-start | bytes 393220
  19.3 198.3 %copy-start.7 = (f32[8,16,1,256]{3,2,1,0:T(1,128)}, f32[8,16,1,256]{3,2,1,0:T(1,128)S(1)}, u32[]{:S(2)}) copy-start(f32[8,16,1,256]{3,2,1,0:T(1,128)S(1)} %get-tuple-element.142) | copy-start | bytes 393220
  19.4 198.3 %copy-start.9 = (f32[8,16,1,256]{3,2,1,0:T(1,128)}, f32[8,16,1,256]{3,2,1,0:T(1,128)S(1)}, u32[]{:S(2)}) copy-start(f32[8,16,1,256]{3,2,1,0:T(1,128)S(1)} %get-tuple-element.145) | copy-start | bytes 393220
  19.4 198.3 %copy-start.11 = (f32[8,16,1,256]{3,2,1,0:T(1,128)}, f32[8,16,1,256]{3,2,1,0:T(1,128)S(1)}, u32[]{:S(2)}) copy-start(f32[8,16,1,256]{3,2,1,0:T(1,128)S(1)} %get-tuple-element.146) | copy-start | bytes 393220
  19.4 199.8 %copy-start.3 = (f32[8,16,1,256]{3,2,1,0:T(1,128)}, f32[8,16,1,256]{3,2,1,0:T(1,128)S(1)}, u32[]{:S(2)}) copy-start(f32[8,16,1,256]{3,2,1,0:T(1,128)S(1)} %get-tuple-element.147) | copy-start | bytes 393220
  200.2 11.5 %copy-start.15 = (f32[8,16,8,256]{3,1,2,0:T(8,128)S(1)}, f32[8,16,8,256]{3,1,2,0:T(8,128)}, u32[]{:S(2)}) copy-start(f32[8,16,8,256]{3,1,2,0:T(8,128)} %copy-done.14) | copy-start | bytes 3145732
  207.0 10.6 copy-start.22
  210.1 7.5 copy-start.23
  213.8 8.7 copy-start.18
  226.6 9.2 copy-start.31
  247.8 7.1 copy-start.42
  247.8 46.9 %copy-start.38 = (s32[256]{0:T(256)S(1)}, s32[256]{0:T(256)}, u32[]{:S(2)}) copy-start(s32[256]{0:T(256)} %copy-done.37) | copy-start | bytes 3076
  344.3 429.2 %all-reduce.8.cloned.1.call-start = ((), (), s32[]{:S(2)}) async-start(), calls=%async_computation.2 | async-start | bytes 4194304 | tf_op jit(solution)/shard_map/psum | solution.py:143
  443.8 240.0 %copy-start.2 = (f32[8,16,8,512]{3,0,2,1:T(8,128)}, f32[8,16,8,512]{3,0,2,1:T(8,128)S(1)}, u32[]{:S(2)}) copy-start(f32[8,16,8,512]{3,0,2,1:T(8,128)S(1)} %multiply_add_fusion) | copy-start | bytes 6291460
  451.6 28.7 %copy-start.51 = (pred[256]{0:T(512)(128)(4,1)S(1)}, pred[256]{0:T(512)(128)(4,1)}, u32[]{:S(2)}) copy-start(pred[256]{0:T(512)(128)(4,1)} %copy-done.50) | copy-start | bytes 772
  473.2 16.0 %copy-start.48 = (pred[256]{0:T(512)(128)(4,1)S(1)}, pred[256]{0:T(512)(128)(4,1)}, u32[]{:S(2)}) copy-start(pred[256]{0:T(512)(128)(4,1)} %copy-done.47) | copy-start | bytes 772
  538.0 8.6 copy-start.32
  579.1 7.1 copy-start.43
  579.1 46.9 %copy-start.39 = (s32[256]{0:T(256)S(1)}, s32[256]{0:T(256)}, u32[]{:S(2)}) copy-start(s32[256]{0:T(256)} %copy-done.37) | copy-start | bytes 3076
  665.8 9.8 copy-start.53
  675.5 139.5 %all-reduce.10.cloned.1.call-start = ((), (), s32[]{:S(2)}) async-start(), calls=%async_computation.3 | async-start | bytes 2097152 | tf_op jit(solution)/shard_map/psum | solution.py:150
  683.8 145.0 %copy-start.35 = (f32[16,4]{0,1:T(4,128)}, f32[16,4]{0,1:T(4,128)S(1)}, u32[]{:S(2)}) copy-start(f32[16,4]{0,1:T(4,128)S(1)} %pad_maximum_fusion) | copy-start | bytes 772
  686.7 344.7 %all-reduce.14.cloned.1.call-start = ((), (), s32[]{:S(2)}) async-start(), calls=%async_computation.5 | async-start | bytes 2097152 | tf_op jit(solution)/shard_map/psum | solution.py:150
  821.1 7.8 copy-start
  828.8 27.8 %copy-start.52 = (pred[256]{0:T(512)(128)(4,1)S(1)}, pred[256]{0:T(512)(128)(4,1)}, u32[]{:S(2)}) copy-start(pred[256]{0:T(512)(128)(4,1)} %copy-done.50) | copy-start | bytes 772
  850.4 13.0 %copy-start.49 = (pred[256]{0:T(512)(128)(4,1)S(1)}, pred[256]{0:T(512)(128)(4,1)}, u32[]{:S(2)}) copy-start(pred[256]{0:T(512)(128)(4,1)} %copy-done.47) | copy-start | bytes 772
  856.7 6.9 copy-start.4
  856.7 6.9 copy-start.6
  856.7 6.9 copy-start.8
  856.7 6.9 copy-start.10
  856.7 6.9 copy-start.12
  875.3 4.7 copy-start.24
  900.9 228.2 %all-reduce.12.cloned.1.call-start = ((), (), s32[]{:S(2)}) async-start(), calls=%async_computation.4 | async-start | bytes 4194304 | tf_op jit(solution)/shard_map/psum | solution.py:143
  908.7 12.5 %copy-start.33 = (f32[8,1,1,256]{3,0,2,1:T(8,128)S(1)}, f32[8,1,1,256]{3,0,2,1:T(8,128)}, u32[]{:S(2)}) copy-start(f32[8,1,1,256]{3,0,2,1:T(8,128)} %copy.581) | copy-start | bytes 24580
  908.7 12.5 %copy-start.19 = (f32[8,1,1,256]{3,0,2,1:T(8,128)S(1)}, f32[8,1,1,256]{3,0,2,1:T(8,128)}, u32[]{:S(2)}) copy-start(f32[8,1,1,256]{3,0,2,1:T(8,128)} %copy.582) | copy-start | bytes 24580
  908.7 12.5 %copy-start.25 = (f32[8,256]{1,0:T(8,128)S(1)}, f32[8,256]{1,0:T(8,128)}, u32[]{:S(2)}) copy-start(f32[8,256]{1,0:T(8,128)} %bitcast_negate_fusion) | copy-start | bytes 24580
  908.7 12.5 %copy-start.26 = (f32[8,256]{1,0:T(8,128)S(1)}, f32[8,256]{1,0:T(8,128)}, u32[]{:S(2)}) copy-start(f32[8,256]{1,0:T(8,128)} %bitcast_negate_fusion.2) | copy-start | bytes 24580
  933.6 7.1 copy-start.44
  933.6 46.9 %copy-start.40 = (s32[256]{0:T(256)S(1)}, s32[256]{0:T(256)}, u32[]{:S(2)}) copy-start(s32[256]{0:T(256)} %copy-done.37) | copy-start | bytes 3076
  1020.3 11.2 copy-start.1
  1020.3 11.2 copy-start.36
  (12 other events, 25.0 us)
Sparse Core Ops, SparseCore 0:
  10.3 129.1 all-gather.1
  344.4 96.5 all-reduce.5
  675.6 97.8 all-reduce.7
  775.6 39.3 all-reduce.9
  901.0 40.0 all-reduce.13
  1030.6 98.4 all-reduce.11
where the time goes:
time: 1150 us; the launch traced here: 1140 us
  waiting for transfers between devices  419 us (36%)
  local copies, waits for them, and re-layouts  357 us (31%)
  other arithmetic  324 us (28%)
  between operations  19.6 us (2%)
  matrix products  18.7 us (2%)
    psum x3, waiting for transfers between devices, per_device(): station_gradients = lax.psum(local_terms, 'base')  258 us
    scatter-add x6, other arithmetic, local_gradients(): gradient_list = jnp.zeros(shape_out, jnp.float32).at[:, :, :, antenna_fir...  239 us
    all_gather x1, waiting for transfers between devices, per_device(): jones_current = lax.all_gather(jones_current, 'base', axis=3, tiled=True)  120 us
    another operation x12, local copies, waits for them, and re-layouts, pack_matrix(): jnp.stack([matrix[0][0][0], matrix[0][0][1], matrix[0][1][0], matrix[0][1...  61.1 us
    gather x6, local copies, waits for them, and re-layouts, per_device(): trailing_rows = jnp.take(jones_current, antenna_second, axis=3)  53.9 us
    gather x6, local copies, waits for them, and re-layouts, per_device(): leading_rows = jnp.take(jones_current, antenna_first, axis=3)  52.7 us
    psum x2, waiting for transfers between devices, per_device(): coefficients = lax.psum(partial_fit, 'band')  41.6 us
    scatter-add x3, local copies, waits for them, and re-layouts, local_gradients(): gradient_list = jnp.zeros(shape_out, jnp.float32).at[:, :, :, antenna_fir...  29.5 us
  transfers between devices with their start and end apart: 6, of which 5 were waited for; matrix products, arithmetic and copies ran while one was open for 15% of the time, Pallas kernels for 0%

commit v1 on v0

--- a/solution.py
+++ b/solution.py
@@ -124,7 +124,7 @@
     local_basis = lax.dynamic_slice_in_dim(poly_basis, lax.axis_index("band") * sub_dev, sub_dev, 0)
     identity = jnp.array([1.0, 0.0, 0.0, 0.0, 0.0, 0.0, 1.0, 0.0], dtype=jnp.float32)[:, None]
     jones_current = identity + jones_deviation
-    jones_current = lax.all_gather(jones_current, "base", axis=3, tiled=True)
+    jones_current = jnp.concatenate(lax.all_gather(jones_current, "base"), axis=3)
     consensus = jones_current
     dual_var = jnp.zeros_like(jones_current)
     residual = None

time: 1150 us -> 1120 us (0.974)
  waiting for transfers between devices: 419 us -> 380 us
    all_gather x1, waiting for transfers between devices: 120 us -> 68.3 us  [per_device(): lax.all_gather(jones_current, 'base')]
    reshape x0 -> x2, local copies, waits for them, and re-layouts: none -> 16.3 us  [per_device(): jnp.concatenate(lax.all_gather(jones_current, 'base'), axis=3)]
    psum x3, waiting for transfers between devices: 258 us -> 270 us  [per_device(): station_gradients = lax.psum(local_terms, 'base')]
    all_gather x2 -> x1, local copies, waits for them, and re-layouts: 23.6 us -> 11.5 us  [per_device(): lax.all_gather(jones_current, 'base')]
  transfers between devices with their start and end apart: 6 -> 6, of which waited for: 5 -> 5; matrix products, arithmetic and copies ran while one was open for 15% -> 14% of each run, Pallas kernels for 0% -> 0%
where the time goes in v1:
time: 1120 us; the launch traced here: 1100 us
  waiting for transfers between devices  380 us (34%)
  local copies, waits for them, and re-layouts  360 us (32%)
  other arithmetic  325 us (29%)
  between operations  19.5 us (2%)
  matrix products  18.7 us (2%)
    psum x3, waiting for transfers between devices, per_device(): station_gradients = lax.psum(local_terms, 'base')  270 us
    scatter-add x6, other arithmetic, local_gradients(): gradient_list = jnp.zeros(shape_out, jnp.float32).at[:, :, :, antenna_fir...  239 us
    all_gather x1, waiting for transfers between devices, per_device(): lax.all_gather(jones_current, 'base')  68.3 us
    another operation x12, local copies, waits for them, and re-layouts, pack_matrix(): jnp.stack([matrix[0][0][0], matrix[0][0][1], matrix[0][1][0], matrix[0][1...  61.1 us
    gather x6, local copies, waits for them, and re-layouts, per_device(): trailing_rows = jnp.take(jones_current, antenna_second, axis=3)  53.8 us
    gather x6, local copies, waits for them, and re-layouts, per_device(): leading_rows = jnp.take(jones_current, antenna_first, axis=3)  52.7 us
    psum x2, waiting for transfers between devices, per_device(): coefficients = lax.psum(partial_fit, 'band')  41.6 us
    scatter-add x3, local copies, waits for them, and re-layouts, local_gradients(): gradient_list = jnp.zeros(shape_out, jnp.float32).at[:, :, :, antenna_fir...  29.5 us
  transfers between devices with their start and end apart: 6, of which 5 were waited for; matrix products, arithmetic and copies ran while one was open for 14% of the time, Pallas kernels for 0%

profile of v1, /device:TPU:0, one launch (start us, length us, event | category | flops | bytes accessed | tf_op | source)
XLA Modules:
  0.0 1104.2 jit_solution(9750144865507982161)
XLA Ops:
  12.6 6.8 fusion.21
  19.4 68.3 %all-gather.3.cloned.1.call-done = f32[128,16,8,32]{3,2,1,0:T(8,128)} async-done(((f32[8,16,8,32]{3,2,1,0:T(8,128)}), f32[128,16,8,32]{3,2,1,0:T(8,128)}) %all-gather.3.cloned.1.call-update) | async-done | bytes 2097168 | tf_op jit(solution)/shard_map/all_gather | solution.py:127
  87.8 11.5 %copy.1186 = f32[16,8,16,8,32]{4,0,1,3,2:T(8,128)} copy(f32[16,8,16,8,32]{4,3,2,1,0:T(8,128)} %bitcast.86) | data formatting | bytes 4194304 | tf_op jit(solution)/shard_map/all_gather | solution.py:127
  99.2 7.5 reshape.185
  106.8 8.7 copy.488
  115.5 10.7 gather_fusion
  126.2 7.1 copy.489
  133.3 10.7 gather_fusion.1
  144.0 7.5 copy.492
  164.8 5.2 fusion.20
  192.8 7.5 copy.518
  204.6 7.7 copy.527
  212.3 7.1 broadcast.414.clone
  219.4 39.8 %scatter_fusion = f32[8,16,8,512]{1,2,3,0:T(8,128)} fusion(f32[8,16,8,512]{1,2,3,0:T(8,128)} %broadcast.414.clone, s32[256]{0:T(256)S(1)} %copy-done.42, f32[256,8,16,8]{2,3,1,0:T(8,128)} %copy.518), kind=kCustom, calls=%fused_computation.6 | custom fusion | flops 262144 | bytes 3146752 | tf_op jit(solution)/shard_map/scatter-add | solution.py:105
  259.2 39.8 %scatter_fusion.1 = f32[8,16,8,512]{1,2,3,0:T(8,128)} fusion(f32[8,16,8,512]{1,2,3,0:T(8,128)} %scatter_fusion, s32[256]{0:T(256)S(1)} %copy-done.38, f32[256,8,16,8]{2,3,1,0:T(8,128)} %copy.527), kind=kCustom, calls=%fused_computation.7 | custom fusion | flops 262144 | bytes 3146752 | tf_op jit(solution)/shard_map/scatter-add | solution.py:107
  299.0 9.7 copy.528
  315.1 90.8 %all-reduce.6.cloned.1.call-done = f32[8,16,8,512]{3,0,2,1:T(8,128)} async-done(((f32[8,16,8,512]{3,0,2,1:T(8,128)}), f32[8,16,8,512]{3,0,2,1:T(8,128)}) %all-reduce.6.cloned.1.call-update) | async-done | bytes 2097168 | tf_op jit(solution)/shard_map/psum | solution.py:143
  408.8 7.8 copy.529
  416.5 10.8 gather_fusion.2
  427.3 10.8 gather_fusion.3
  438.1 7.1 copy.530
  446.6 7.5 copy.532
  470.3 5.2 fusion.19
  516.1 7.5 copy.551
  536.3 7.7 copy.560
  544.0 7.1 broadcast.414.clone.1
  551.1 39.8 %scatter_fusion.2 = f32[8,16,8,512]{1,2,3,0:T(8,128)} fusion(f32[8,16,8,512]{1,2,3,0:T(8,128)} %broadcast.414.clone.1, s32[256]{0:T(256)S(1)} %copy-done.43, f32[256,8,16,8]{2,3,1,0:T(8,128)} %copy.551), kind=kCustom, calls=%fused_computation.8 | custom fusion | flops 262144 | bytes 3146752 | tf_op jit(solution)/shard_map/scatter-add | solution.py:105
  590.8 39.8 %scatter_fusion.3 = f32[8,16,8,512]{1,2,3,0:T(8,128)} fusion(f32[8,16,8,512]{1,2,3,0:T(8,128)} %scatter_fusion.2, s32[256]{0:T(256)S(1)} %copy-done.39, f32[256,8,16,8]{2,3,1,0:T(8,128)} %copy.560), kind=kCustom, calls=%fused_computation.9 | custom fusion | flops 262144 | bytes 3146752 | tf_op jit(solution)/shard_map/scatter-add | solution.py:107
  630.6 9.7 copy.561
  651.8 86.5 %all-reduce.8.cloned.1.call-done = f32[8,16,8,512]{3,0,2,1:T(8,128)} async-done(((f32[8,16,8,512]{3,0,2,1:T(8,128)}), f32[8,16,8,512]{3,0,2,1:T(8,128)}) %all-reduce.8.cloned.1.call-update) | async-done | bytes 2097168 | tf_op jit(solution)/shard_map/psum | solution.py:143
  738.3 41.6 %all-reduce.10.cloned.1.call-done = f32[4,16,8,512]{3,0,2,1:T(4,128)} async-done(((f32[4,16,8,512]{3,0,2,1:T(4,128)}), f32[4,16,8,512]{3,0,2,1:T(4,128)}) %all-reduce.10.cloned.1.call-update) | async-done | bytes 1048592 | tf_op jit(solution)/shard_map/psum | solution.py:150
  779.9 6.0 broadcast_multiply_fusion
  785.9 7.8 copy.562
  793.6 10.8 gather_fusion.4
  804.5 10.8 gather_fusion.5
  815.2 6.3 copy.563
  821.7 6.6 copy.565
  833.3 5.3 fusion.18
  860.7 5.1 fusion.2
  873.6 4.1 stack.31
  877.7 8.4 copy.584
  891.0 7.5 copy.593
  898.5 7.1 broadcast.414
  905.6 39.8 %scatter_fusion.4 = f32[8,16,8,512]{1,2,3,0:T(8,128)} fusion(f32[8,16,8,512]{1,2,3,0:T(8,128)} %broadcast.414, s32[256]{0:T(256)S(1)} %copy-done.44, f32[256,8,16,8]{2,3,1,0:T(8,128)} %copy.584), kind=kCustom, calls=%fused_computation.10 | custom fusion | flops 262144 | bytes 3146752 | tf_op jit(solution)/shard_map/scatter-add | solution.py:105
  945.4 39.8 %scatter_fusion.5 = f32[8,16,8,512]{1,2,3,0:T(8,128)} fusion(f32[8,16,8,512]{1,2,3,0:T(8,128)} %scatter_fusion.4, s32[256]{0:T(256)S(1)} %copy-done.40, f32[256,8,16,8]{2,3,1,0:T(8,128)} %copy.593), kind=kCustom, calls=%fused_computation.11 | custom fusion | flops 262144 | bytes 3146752 | tf_op jit(solution)/shard_map/scatter-add | solution.py:107
  985.2 10.1 copy.594
  996.3 4.8 convolution_subtract_fusion
  1001.2 92.8 %all-reduce.12.cloned.1.call-done = f32[8,16,8,512]{3,0,2,1:T(8,128)} async-done(((f32[8,16,8,512]{3,0,2,1:T(8,128)}), f32[8,16,8,512]{3,0,2,1:T(8,128)}) %all-reduce.12.cloned.1.call-update) | async-done | bytes 2097168 | tf_op jit(solution)/shard_map/psum | solution.py:143
  (289 shorter events, 176.7 us)
Async XLA Ops:
  7.2 80.6 %all-gather.3.cloned.1.call-start = ((), (), s32[]{:S(2)}) async-start(), calls=%async_computation.5 | async-start | bytes 8912896 | tf_op jit(solution)/shard_map/all_gather | solution.py:127
  9.2 396.7 %all-reduce.6.cloned.1.call-start = ((), (), s32[]{:S(2)}) async-start(), calls=%async_computation | async-start | bytes 4194304 | tf_op jit(solution)/shard_map/psum | solution.py:143
  10.5 152.9 %copy-start.13 = (f32[8,8,256]{1,0,2:T(8,128)}, f32[8,8,256]{1,0,2:T(8,128)S(1)}, u32[]{:S(2)}) copy-start(f32[8,8,256]{1,0,2:T(8,128)S(1)} %copy.501) | copy-start | bytes 196612
  11.3 104.2 %copy-start.45 = (s32[1024]{0:T(1024)}, s32[1024]{0:T(1024)S(1)}, u32[]{:S(2)}) copy-start(s32[1024]{0:T(1024)S(1)} %pad_clamp_fusion.1) | copy-start | bytes 12292
  11.9 121.4 %copy-start.46 = (s32[1024]{0:T(1024)}, s32[1024]{0:T(1024)S(1)}, u32[]{:S(2)}) copy-start(s32[1024]{0:T(1024)S(1)} %pad_clamp_fusion) | copy-start | bytes 12292
  12.6 138.9 %copy-start.50 = (pred[256]{0:T(512)(128)(4,1)}, pred[256]{0:T(512)(128)(4,1)S(1)}, u32[]{:S(2)}) copy-start(pred[256]{0:T(512)(128)(4,1)S(1)} %get-tuple-element.206) | copy-start | bytes 772
  12.6 140.3 %copy-start.47 = (pred[256]{0:T(512)(128)(4,1)}, pred[256]{0:T(512)(128)(4,1)S(1)}, u32[]{:S(2)}) copy-start(pred[256]{0:T(512)(128)(4,1)S(1)} %get-tuple-element.205) | copy-start | bytes 772
  19.4 162.8 %copy-start.5 = (f32[8,16,1,256]{3,2,1,0:T(1,128)}, f32[8,16,1,256]{3,2,1,0:T(1,128)S(1)}, u32[]{:S(2)}) copy-start(f32[8,16,1,256]{3,2,1,0:T(1,128)S(1)} %get-tuple-element.140) | copy-start | bytes 393220
  19.4 162.8 %copy-start.7 = (f32[8,16,1,256]{3,2,1,0:T(1,128)}, f32[8,16,1,256]{3,2,1,0:T(1,128)S(1)}, u32[]{:S(2)}) copy-start(f32[8,16,1,256]{3,2,1,0:T(1,128)S(1)} %get-tuple-element.142) | copy-start | bytes 393220
  19.4 162.8 %copy-start.9 = (f32[8,16,1,256]{3,2,1,0:T(1,128)}, f32[8,16,1,256]{3,2,1,0:T(1,128)S(1)}, u32[]{:S(2)}) copy-start(f32[8,16,1,256]{3,2,1,0:T(1,128)S(1)} %get-tuple-element.145) | copy-start | bytes 393220
  19.4 162.8 %copy-start.11 = (f32[8,16,1,256]{3,2,1,0:T(1,128)}, f32[8,16,1,256]{3,2,1,0:T(1,128)S(1)}, u32[]{:S(2)}) copy-start(f32[8,16,1,256]{3,2,1,0:T(1,128)S(1)} %get-tuple-element.146) | copy-start | bytes 393220
  19.4 164.3 %copy-start.3 = (f32[8,16,1,256]{3,2,1,0:T(1,128)}, f32[8,16,1,256]{3,2,1,0:T(1,128)S(1)}, u32[]{:S(2)}) copy-start(f32[8,16,1,256]{3,2,1,0:T(1,128)S(1)} %get-tuple-element.147) | copy-start | bytes 393220
  164.8 11.5 %copy-start.15 = (f32[8,16,8,256]{3,1,2,0:T(8,128)S(1)}, f32[8,16,8,256]{3,1,2,0:T(8,128)}, u32[]{:S(2)}) copy-start(f32[8,16,8,256]{3,1,2,0:T(8,128)} %copy-done.14) | copy-start | bytes 3145732
  171.5 10.6 copy-start.22
  174.7 7.5 copy-start.23
  178.4 8.7 copy-start.18
  191.1 9.2 copy-start.31
  212.3 7.1 copy-start.42
  212.3 46.9 %copy-start.38 = (s32[256]{0:T(256)S(1)}, s32[256]{0:T(256)}, u32[]{:S(2)}) copy-start(s32[256]{0:T(256)} %copy-done.37) | copy-start | bytes 3076
  308.7 429.6 %all-reduce.8.cloned.1.call-start = ((), (), s32[]{:S(2)}) async-start(), calls=%async_computation.1 | async-start | bytes 4194304 | tf_op jit(solution)/shard_map/psum | solution.py:143
  408.7 240.1 %copy-start.2 = (f32[8,16,8,512]{3,0,2,1:T(8,128)}, f32[8,16,8,512]{3,0,2,1:T(8,128)S(1)}, u32[]{:S(2)}) copy-start(f32[8,16,8,512]{3,0,2,1:T(8,128)S(1)} %multiply_add_fusion) | copy-start | bytes 6291460
  416.5 28.7 %copy-start.51 = (pred[256]{0:T(512)(128)(4,1)S(1)}, pred[256]{0:T(512)(128)(4,1)}, u32[]{:S(2)}) copy-start(pred[256]{0:T(512)(128)(4,1)} %copy-done.50) | copy-start | bytes 772
  438.1 16.0 %copy-start.48 = (pred[256]{0:T(512)(128)(4,1)S(1)}, pred[256]{0:T(512)(128)(4,1)}, u32[]{:S(2)}) copy-start(pred[256]{0:T(512)(128)(4,1)} %copy-done.47) | copy-start | bytes 772
  502.9 8.6 copy-start.32
  544.0 7.1 copy-start.43
  544.0 46.9 %copy-start.39 = (s32[256]{0:T(256)S(1)}, s32[256]{0:T(256)}, u32[]{:S(2)}) copy-start(s32[256]{0:T(256)} %copy-done.37) | copy-start | bytes 3076
  630.6 9.8 copy-start.53
  640.3 139.5 %all-reduce.10.cloned.1.call-start = ((), (), s32[]{:S(2)}) async-start(), calls=%async_computation.2 | async-start | bytes 2097152 | tf_op jit(solution)/shard_map/psum | solution.py:150
  648.9 144.8 %copy-start.35 = (f32[16,4]{0,1:T(4,128)}, f32[16,4]{0,1:T(4,128)S(1)}, u32[]{:S(2)}) copy-start(f32[16,4]{0,1:T(4,128)S(1)} %pad_maximum_fusion) | copy-start | bytes 772
  651.7 344.6 %all-reduce.14.cloned.1.call-start = ((), (), s32[]{:S(2)}) async-start(), calls=%async_computation.4 | async-start | bytes 2097152 | tf_op jit(solution)/shard_map/psum | solution.py:150
  785.9 7.8 copy-start
  793.6 27.8 %copy-start.52 = (pred[256]{0:T(512)(128)(4,1)S(1)}, pred[256]{0:T(512)(128)(4,1)}, u32[]{:S(2)}) copy-start(pred[256]{0:T(512)(128)(4,1)} %copy-done.50) | copy-start | bytes 772
  815.2 13.0 %copy-start.49 = (pred[256]{0:T(512)(128)(4,1)S(1)}, pred[256]{0:T(512)(128)(4,1)}, u32[]{:S(2)}) copy-start(pred[256]{0:T(512)(128)(4,1)} %copy-done.47) | copy-start | bytes 772
  821.5 6.9 copy-start.4
  821.5 6.9 copy-start.6
  821.5 6.9 copy-start.8
  821.5 6.9 copy-start.10
  821.5 6.9 copy-start.12
  840.1 4.7 copy-start.24
  865.7 228.2 %all-reduce.12.cloned.1.call-start = ((), (), s32[]{:S(2)}) async-start(), calls=%async_computation.3 | async-start | bytes 4194304 | tf_op jit(solution)/shard_map/psum | solution.py:143
  873.6 12.5 %copy-start.33 = (f32[8,1,1,256]{3,0,2,1:T(8,128)S(1)}, f32[8,1,1,256]{3,0,2,1:T(8,128)}, u32[]{:S(2)}) copy-start(f32[8,1,1,256]{3,0,2,1:T(8,128)} %copy.569) | copy-start | bytes 24580
  873.6 12.5 %copy-start.19 = (f32[8,1,1,256]{3,0,2,1:T(8,128)S(1)}, f32[8,1,1,256]{3,0,2,1:T(8,128)}, u32[]{:S(2)}) copy-start(f32[8,1,1,256]{3,0,2,1:T(8,128)} %copy.570) | copy-start | bytes 24580
  873.6 12.5 %copy-start.25 = (f32[8,256]{1,0:T(8,128)S(1)}, f32[8,256]{1,0:T(8,128)}, u32[]{:S(2)}) copy-start(f32[8,256]{1,0:T(8,128)} %bitcast_negate_fusion) | copy-start | bytes 24580
  873.6 12.5 %copy-start.26 = (f32[8,256]{1,0:T(8,128)S(1)}, f32[8,256]{1,0:T(8,128)}, u32[]{:S(2)}) copy-start(f32[8,256]{1,0:T(8,128)} %bitcast_negate_fusion.2) | copy-start | bytes 24580
  898.5 7.1 copy-start.44
  898.5 46.9 %copy-start.40 = (s32[256]{0:T(256)S(1)}, s32[256]{0:T(256)}, u32[]{:S(2)}) copy-start(s32[256]{0:T(256)} %copy-done.37) | copy-start | bytes 3076
  985.2 11.2 %copy-start.1 = (f32[8,16,8,512]{3,0,2,1:T(8,128)S(1)}, f32[8,16,8,512]{3,0,2,1:T(8,128)}, u32[]{:S(2)}) copy-start(f32[8,16,8,512]{3,0,2,1:T(8,128)} %copy-done) | copy-start | bytes 6291460
  985.2 11.2 %copy-start.36 = (f32[16,4]{0,1:T(4,128)S(1)}, f32[16,4]{0,1:T(4,128)}, u32[]{:S(2)}) copy-start(f32[16,4]{0,1:T(4,128)} %copy-done.35) | copy-start | bytes 772
  (12 other events, 25.0 us)
Sparse Core Ops, SparseCore 0:
  10.7 77.0 all-gather.2
  308.8 97.0 all-reduce.5
  640.4 97.8 all-reduce.7
  740.4 39.3 all-reduce.9
  865.9 40.0 all-reduce.13
  995.4 98.4 all-reduce.11
